TPU v7x, 32 devices: a whole 2x2x4 slice. The times are simulated.
32 devices in a mesh: dp: 8 (over y, x, core), seq: 4 (over z).
Axes of the slice: x: 2, y: 2, z: 4, core: 2. Of those that a mesh axis runs over, the one named last changes fastest.
Arguments:
- inputs: bfloat16 [24, 1024, 768], P('dp', 'seq'), may hold values from -6 to 6
- segment_ids: int32 [24, 1024], P('dp', 'seq'), may hold values from 0 to 3, never falling along the last dimension, each value on 1 to 512 neighbouring positions
- norm1_gain: bfloat16 [768], P('dp'), may hold values from 0.5 to 1.5
- norm1_shift: bfloat16 [768], P('dp'), may hold values from -1.5 to 1.5
- query_weight: bfloat16 [768, 768], P('dp'), may hold values from -0.4375 to 0.4375
- query_bias: bfloat16 [768], P('dp'), may hold values from -2.5 to 2.5
- key_weight: bfloat16 [768, 768], P('dp'), may hold values from -0.21875 to 0.21875
- value_weight: bfloat16 [768, 768], P('dp'), may hold values from -0.21875 to 0.21875
- value_bias: bfloat16 [768], P('dp'), may hold values from -1.5 to 1.5
- out_weight: bfloat16 [768, 768], P('dp'), may hold values from -0.625 to 0.625
- out_bias: bfloat16 [768], P('dp'), may hold values from -1.5 to 1.5
- norm2_gain: bfloat16 [768], P('dp'), may hold values from 0.5 to 1.5
- norm2_shift: bfloat16 [768], P('dp'), may hold values from -1.5 to 1.5
- fc1_weight: bfloat16 [768, 3072], P('dp'), may hold values from -0.21875 to 0.21875
- fc1_bias: bfloat16 [3072], P('dp'), may hold values from -1.5 to 1.5
- fc2_weight: bfloat16 [3072, 768], P('dp'), may hold values from -0.15625 to 0.15625
- fc2_bias: bfloat16 [768], P('dp'), may hold values from -1.5 to 1.5
- grad_output: bfloat16 [24, 1024, 768], P('dp', 'seq'), may hold values from -6 to 6
Outputs:
- output: bfloat16 [24, 1024, 768], P('dp', 'seq')
- grad_inputs: bfloat16 [24, 1024, 768], P('dp', 'seq')
- grad_norm1_gain: float32 [768], P('dp')
- grad_norm1_shift: float32 [768], P('dp')
- grad_query_weight: float32 [768, 768], P('dp')
- grad_query_bias: float32 [768], P('dp')
- grad_key_weight: float32 [768, 768], P('dp')
- grad_value_weight: float32 [768, 768], P('dp')
- grad_value_bias: float32 [768], P('dp')
- grad_out_weight: float32 [768, 768], P('dp')
- grad_out_bias: float32 [768], P('dp')
- grad_norm2_gain: float32 [768], P('dp')
- grad_norm2_shift: float32 [768], P('dp')
- grad_fc1_weight: float32 [768, 3072], P('dp')
- grad_fc1_bias: float32 [3072], P('dp')
- grad_fc2_weight: float32 [3072, 768], P('dp')
- grad_fc2_bias: float32 [768], P('dp')
Inputs may be any that keep to these rules, and one draw needn't show every extreme that they name: `segment_ids`: within each sequence, segment numbers never fall along the positions; each segment is a run of 1 to 512 positions.
All inputs are finite; a program needn't handle non-finite values.
Results may differ from a plain program's by a relative error of at most 0.017.
Values may be sent and summed in bfloat16 or wider, within the bound.
No kernel may reach another device: no remote copies, remote signals or barrier semaphores. Data moves between devices by JAX's collectives and lax.ppermute only.
A program may use at most 192 MiB of HBM per device.

v0:
```python
import jax
import jax.numpy as jnp
from jax import lax
from jax.sharding import PartitionSpec as P

HD = 64
EPSILON = 1e-05


def layer_norm(values, gain, shift):
    center = values - jnp.mean(values, axis=-1, keepdims=True)
    inverse = lax.rsqrt(jnp.mean(center * center, axis=-1, keepdims=True) + EPSILON)
    normed = center * inverse
    return (normed * gain + shift, normed, inverse)


def norm_back(grad, normed, inverse, gain):
    scaled = grad * gain
    return inverse * (
        scaled
        - jnp.mean(scaled, axis=-1, keepdims=True)
        - normed * jnp.mean(scaled * normed, axis=-1, keepdims=True)
    )


def gelu_slope(pre_act):
    return (
        0.5 * (1.0 + lax.erf(pre_act * 0.7071067811865476))
        + pre_act * jnp.exp(-0.5 * pre_act * pre_act) * 0.3989422804014327
    )


def cross_rows(left, right):
    return lax.dot_general(
        left, right, (((0,), (0,)), ((), ())), preferred_element_type=jnp.float32
    )


def times_transpose(left, right):
    return lax.dot_general(
        left, right, (((1,), (1,)), ((), ())), preferred_element_type=jnp.float32
    )


def to_pairs(array, heads_here):
    seqs_here, positions, _ = array.shape
    shaped = array.reshape(seqs_here, positions, heads_here, HD).transpose(0, 2, 1, 3)
    return shaped.reshape(seqs_here * heads_here, positions, HD)


def from_pairs(array, seqs_here, heads_here):
    positions = array.shape[1]
    shaped = array.reshape(seqs_here, heads_here, positions, HD).transpose(0, 2, 1, 3)
    return shaped.reshape(seqs_here, positions, heads_here * HD)


def masked_scores(query_pair, key_pair, segment_row):
    scores = jnp.einsum(
        "qd,kd->qk", query_pair, key_pair, preferred_element_type=jnp.float32
    ) * HD ** (-0.5)
    same_segment = segment_row[:, None] == segment_row[None, :]
    return jnp.where(same_segment, scores, -1e30)


def attend_forward(packed):
    query_pair, key_pair, value_pair, segment_row = packed
    scores = masked_scores(query_pair, key_pair, segment_row)
    highest = jnp.max(scores, axis=-1, keepdims=True)
    expon = jnp.exp(scores - highest)
    totals = jnp.sum(expon, axis=-1, keepdims=True)
    probs = (expon / totals).astype(jnp.bfloat16)
    result = jnp.dot(probs, value_pair, preferred_element_type=jnp.float32).astype(jnp.bfloat16)
    return (result, (highest + jnp.log(totals))[:, 0])


def attend_backward(packed):
    query_pair, key_pair, value_pair, segment_row, logsum, grad_pair = packed
    scores = masked_scores(query_pair, key_pair, segment_row)
    probs = jnp.exp(scores - logsum[:, None])
    grad_probs = jnp.einsum("qd,kd->qk", grad_pair, value_pair, preferred_element_type=jnp.float32)
    delta = jnp.sum(probs * grad_probs, axis=-1, keepdims=True)
    grad_scores = (probs * (grad_probs - delta)).astype(jnp.bfloat16)
    factor = HD ** (-0.5)
    grad_query = (
        jnp.einsum("qk,kd->qd", grad_scores, key_pair, preferred_element_type=jnp.float32) * factor
    ).astype(jnp.bfloat16)
    grad_key = (
        jnp.einsum("qk,qd->kd", grad_scores, query_pair, preferred_element_type=jnp.float32)
        * factor
    ).astype(jnp.bfloat16)
    grad_value = jnp.einsum(
        "qk,qd->kd", probs.astype(jnp.bfloat16), grad_pair, preferred_element_type=jnp.float32
    ).astype(jnp.bfloat16)
    return (grad_query, grad_key, grad_value)


def column_sum(array):
    return jnp.sum(array.astype(jnp.float32), axis=0)


def per_device(
    inputs,
    segment_ids,
    norm1_gain,
    norm1_shift,
    query_weight,
    query_bias,
    key_weight,
    value_weight,
    value_bias,
    out_weight,
    out_bias,
    norm2_gain,
    norm2_shift,
    fc1_weight,
    fc1_bias,
    fc2_weight,
    fc2_bias,
    grad_output,
):
    seqs_here, positions, model_width = inputs.shape
    token_rows = seqs_here * positions
    (
        first_gain,
        first_shift,
        w_query,
        b_query,
        w_key,
        w_value,
        b_value,
        w_out,
        b_out,
        second_gain,
        second_shift,
        w_up,
        b_up,
        w_down,
        b_down,
    ) = (
        lax.all_gather(norm1_gain, "dp", axis=0, tiled=True),
        lax.all_gather(norm1_shift, "dp", axis=0, tiled=True),
        lax.all_gather(query_weight, "dp", axis=0, tiled=True),
        lax.all_gather(query_bias, "dp", axis=0, tiled=True),
        lax.all_gather(key_weight, "dp", axis=0, tiled=True),
        lax.all_gather(value_weight, "dp", axis=0, tiled=True),
        lax.all_gather(value_bias, "dp", axis=0, tiled=True),
        lax.all_gather(out_weight, "dp", axis=0, tiled=True),
        lax.all_gather(out_bias, "dp", axis=0, tiled=True),
        lax.all_gather(norm2_gain, "dp", axis=0, tiled=True),
        lax.all_gather(norm2_shift, "dp", axis=0, tiled=True),
        lax.all_gather(fc1_weight, "dp", axis=0, tiled=True),
        lax.all_gather(fc1_bias, "dp", axis=0, tiled=True),
        lax.all_gather(fc2_weight, "dp", axis=0, tiled=True),
        lax.all_gather(fc2_bias, "dp", axis=0, tiled=True),
    )
    full_segments = lax.all_gather(segment_ids, "seq", axis=1, tiled=True)
    flat_in = inputs.reshape(token_rows, model_width).astype(jnp.float32)
    normed_one, unit_one, inverse_one = layer_norm(
        flat_in, first_gain.astype(jnp.float32), first_shift.astype(jnp.float32)
    )
    act_one = normed_one.astype(jnp.bfloat16)
    query_tok = (
        jnp.dot(act_one, w_query, preferred_element_type=jnp.float32) + b_query.astype(jnp.float32)
    ).astype(jnp.bfloat16)
    key_tok = jnp.dot(act_one, w_key, preferred_element_type=jnp.float32).astype(jnp.bfloat16)
    value_tok = (
        jnp.dot(act_one, w_value, preferred_element_type=jnp.float32) + b_value.astype(jnp.float32)
    ).astype(jnp.bfloat16)
    query_heads, key_heads, value_heads = (
        lax.all_to_all(
            query_tok.reshape(seqs_here, positions, model_width),
            "seq",
            split_axis=2,
            concat_axis=1,
            tiled=True,
        ),
        lax.all_to_all(
            key_tok.reshape(seqs_here, positions, model_width),
            "seq",
            split_axis=2,
            concat_axis=1,
            tiled=True,
        ),
        lax.all_to_all(
            value_tok.reshape(seqs_here, positions, model_width),
            "seq",
            split_axis=2,
            concat_axis=1,
            tiled=True,
        ),
    )
    heads_here = query_heads.shape[2] // HD
    query_pairs = to_pairs(query_heads, heads_here)
    key_pairs = to_pairs(key_heads, heads_here)
    value_pairs = to_pairs(value_heads, heads_here)
    segment_pairs = jnp.repeat(full_segments, heads_here, axis=0)
    attn_pairs, logsum = lax.map(
        attend_forward, (query_pairs, key_pairs, value_pairs, segment_pairs)
    )
    attn_heads = from_pairs(attn_pairs, seqs_here, heads_here)
    attn_tok = lax.all_to_all(attn_heads, "seq", split_axis=1, concat_axis=2, tiled=True).reshape(
        token_rows, model_width
    )
    middle = (
        flat_in
        + jnp.dot(attn_tok, w_out, preferred_element_type=jnp.float32)
        + b_out.astype(jnp.float32)
    )
    normed_two, unit_two, inverse_two = layer_norm(
        middle, second_gain.astype(jnp.float32), second_shift.astype(jnp.float32)
    )
    act_two = normed_two.astype(jnp.bfloat16)
    pre_act = jnp.dot(act_two, w_up, preferred_element_type=jnp.float32) + b_up.astype(jnp.float32)
    hidden = jax.nn.gelu(pre_act, approximate=False).astype(jnp.bfloat16)
    result = (
        middle
        + jnp.dot(hidden, w_down, preferred_element_type=jnp.float32)
        + b_down.astype(jnp.float32)
    )
    output = result.astype(jnp.bfloat16).reshape(seqs_here, positions, model_width)
    first_gain_b, w_query_b, w_key_b, w_value_b, w_out_b, second_gain_b, w_up_b, w_down_b = (
        lax.all_gather(norm1_gain, "dp", axis=0, tiled=True),
        lax.all_gather(query_weight, "dp", axis=0, tiled=True),
        lax.all_gather(key_weight, "dp", axis=0, tiled=True),
        lax.all_gather(value_weight, "dp", axis=0, tiled=True),
        lax.all_gather(out_weight, "dp", axis=0, tiled=True),
        lax.all_gather(norm2_gain, "dp", axis=0, tiled=True),
        lax.all_gather(fc1_weight, "dp", axis=0, tiled=True),
        lax.all_gather(fc2_weight, "dp", axis=0, tiled=True),
    )
    grad_down = grad_output.reshape(token_rows, model_width)
    d_b_down = column_sum(grad_down)
    d_w_down = cross_rows(hidden, grad_down)
    grad_hidden = times_transpose(grad_down, w_down_b)
    grad_pre = (grad_hidden * gelu_slope(pre_act)).astype(jnp.bfloat16)
    d_b_up = column_sum(grad_pre)
    d_w_up = cross_rows(act_two, grad_pre)
    grad_two = times_transpose(grad_pre, w_up_b)
    d_second_gain = jnp.sum(grad_two * unit_two, axis=0)
    d_second_shift = jnp.sum(grad_two, axis=0)
    grad_middle = grad_down.astype(jnp.float32) + norm_back(
        grad_two, unit_two, inverse_two, second_gain_b.astype(jnp.float32)
    )
    grad_branch = grad_middle.astype(jnp.bfloat16)
    d_b_out = column_sum(grad_branch)
    d_w_out = cross_rows(attn_tok, grad_branch)
    grad_attn = (
        times_transpose(grad_branch, w_out_b)
        .astype(jnp.bfloat16)
        .reshape(seqs_here, positions, model_width)
    )
    grad_attn_heads = lax.all_to_all(grad_attn, "seq", split_axis=2, concat_axis=1, tiled=True)
    grad_query_pairs, grad_key_pairs, grad_value_pairs = lax.map(
        attend_backward,
        (
            query_pairs,
            key_pairs,
            value_pairs,
            segment_pairs,
            logsum,
            to_pairs(grad_attn_heads, heads_here),
        ),
    )
    grad_query_tok, grad_key_tok, grad_value_tok = (
        lax.all_to_all(
            from_pairs(grad_query_pairs, seqs_here, heads_here),
            "seq",
            split_axis=1,
            concat_axis=2,
            tiled=True,
        ),
        lax.all_to_all(
            from_pairs(grad_key_pairs, seqs_here, heads_here),
            "seq",
            split_axis=1,
            concat_axis=2,
            tiled=True,
        ),
        lax.all_to_all(
            from_pairs(grad_value_pairs, seqs_here, heads_here),
            "seq",
            split_axis=1,
            concat_axis=2,
            tiled=True,
        ),
    )
    grad_query_tok = grad_query_tok.reshape(token_rows, model_width)
    grad_key_tok = grad_key_tok.reshape(token_rows, model_width)
    grad_value_tok = grad_value_tok.reshape(token_rows, model_width)
    d_b_query = column_sum(grad_query_tok)
    d_b_value = column_sum(grad_value_tok)
    d_w_query = cross_rows(act_one, grad_query_tok)
    d_w_key = cross_rows(act_one, grad_key_tok)
    d_w_value = cross_rows(act_one, grad_value_tok)
    grad_one = (
        times_transpose(grad_query_tok, w_query_b)
        + times_transpose(grad_key_tok, w_key_b)
        + times_transpose(grad_value_tok, w_value_b)
    )
    d_first_gain = jnp.sum(grad_one * unit_one, axis=0)
    d_first_shift = jnp.sum(grad_one, axis=0)
    grad_inputs = grad_middle + norm_back(
        grad_one, unit_one, inverse_one, first_gain_b.astype(jnp.float32)
    )
    grad_inputs = grad_inputs.astype(jnp.bfloat16).reshape(seqs_here, positions, model_width)
    (
        part_first_gain,
        part_first_shift,
        part_w_query,
        part_b_query,
        part_w_key,
        part_w_value,
        part_b_value,
        part_w_out,
        part_b_out,
        part_second_gain,
        part_second_shift,
        part_w_up,
        part_b_up,
        part_w_down,
        part_b_down,
    ) = (
        lax.psum_scatter(d_first_gain, "dp", scatter_dimension=0, tiled=True),
        lax.psum_scatter(d_first_shift, "dp", scatter_dimension=0, tiled=True),
        lax.psum_scatter(d_w_query, "dp", scatter_dimension=0, tiled=True),
        lax.psum_scatter(d_b_query, "dp", scatter_dimension=0, tiled=True),
        lax.psum_scatter(d_w_key, "dp", scatter_dimension=0, tiled=True),
        lax.psum_scatter(d_w_value, "dp", scatter_dimension=0, tiled=True),
        lax.psum_scatter(d_b_value, "dp", scatter_dimension=0, tiled=True),
        lax.psum_scatter(d_w_out, "dp", scatter_dimension=0, tiled=True),
        lax.psum_scatter(d_b_out, "dp", scatter_dimension=0, tiled=True),
        lax.psum_scatter(d_second_gain, "dp", scatter_dimension=0, tiled=True),
        lax.psum_scatter(d_second_shift, "dp", scatter_dimension=0, tiled=True),
        lax.psum_scatter(d_w_up, "dp", scatter_dimension=0, tiled=True),
        lax.psum_scatter(d_b_up, "dp", scatter_dimension=0, tiled=True),
        lax.psum_scatter(d_w_down, "dp", scatter_dimension=0, tiled=True),
        lax.psum_scatter(d_b_down, "dp", scatter_dimension=0, tiled=True),
    )
    (
        shard_first_gain,
        shard_first_shift,
        shard_w_query,
        shard_b_query,
        shard_w_key,
        shard_w_value,
        shard_b_value,
        shard_w_out,
        shard_b_out,
        shard_second_gain,
        shard_second_shift,
        shard_w_up,
        shard_b_up,
        shard_w_down,
        shard_b_down,
    ) = (
        lax.psum(part_first_gain.astype(jnp.bfloat16), "seq").astype(jnp.float32),
        lax.psum(part_first_shift.astype(jnp.bfloat16), "seq").astype(jnp.float32),
        lax.psum(part_w_query.astype(jnp.bfloat16), "seq").astype(jnp.float32),
        lax.psum(part_b_query.astype(jnp.bfloat16), "seq").astype(jnp.float32),
        lax.psum(part_w_key.astype(jnp.bfloat16), "seq").astype(jnp.float32),
        lax.psum(part_w_value.astype(jnp.bfloat16), "seq").astype(jnp.float32),
        lax.psum(part_b_value.astype(jnp.bfloat16), "seq").astype(jnp.float32),
        lax.psum(part_w_out.astype(jnp.bfloat16), "seq").astype(jnp.float32),
        lax.psum(part_b_out.astype(jnp.bfloat16), "seq").astype(jnp.float32),
        lax.psum(part_second_gain.astype(jnp.bfloat16), "seq").astype(jnp.float32),
        lax.psum(part_second_shift.astype(jnp.bfloat16), "seq").astype(jnp.float32),
        lax.psum(part_w_up.astype(jnp.bfloat16), "seq").astype(jnp.float32),
        lax.psum(part_b_up.astype(jnp.bfloat16), "seq").astype(jnp.float32),
        lax.psum(part_w_down.astype(jnp.bfloat16), "seq").astype(jnp.float32),
        lax.psum(part_b_down.astype(jnp.bfloat16), "seq").astype(jnp.float32),
    )
    return (
        output,
        grad_inputs,
        shard_first_gain,
        shard_first_shift,
        shard_w_query,
        shard_b_query,
        shard_w_key,
        shard_w_value,
        shard_b_value,
        shard_w_out,
        shard_b_out,
        shard_second_gain,
        shard_second_shift,
        shard_w_up,
        shard_b_up,
        shard_w_down,
        shard_b_down,
    )


def solution(mesh):
    placed = (
        P("dp", "seq", None),
        P("dp", "seq"),
        P("dp"),
        P("dp"),
        P("dp", None),
        P("dp"),
        P("dp", None),
        P("dp", None),
        P("dp"),
        P("dp", None),
        P("dp"),
        P("dp"),
        P("dp"),
        P("dp", None),
        P("dp"),
        P("dp", None),
        P("dp"),
        P("dp", "seq", None),
    )
    return jax.shard_map(
        per_device,
        mesh=mesh,
        in_specs=placed,
        out_specs=(
            P("dp", "seq", None),
            P("dp", "seq", None),
            P("dp"),
            P("dp"),
            P("dp", None),
            P("dp"),
            P("dp", None),
            P("dp", None),
            P("dp"),
            P("dp", None),
            P("dp"),
            P("dp"),
            P("dp"),
            P("dp", None),
            P("dp"),
            P("dp", None),
            P("dp"),
        ),
        check_vma=False,
    )
```

profile of v0, /device:TPU:0, one launch (start us, length us, event | category | flops | bytes accessed | tf_op | source)
XLA Modules:
  0.0 1093.1 jit_solution(9284306337476619404)
XLA Ops:
  15.2 26.3 %all-reduce.18 = (bf16[768]{0:T(1024)(128)(2,1)S(1)}, bf16[768]{0:T(1024)(128)(2,1)S(1)}, bf16[768]{0:T(1024)(128)(2,1)S(1)}, bf16[768]{0:T(1024)(128)(2,1)S(1)}...) all-reduce(bf16[768]{0:T(1024)(128)(2,1)S(1)} %dynamic-update-slice, ...), channel_id=1, replica_groups=mesh['dp'=8,'seq'=4] {'dp'}, use_global_device_ids=true, to_apply=%add.1 | all-reduce | flops 6144 | bytes 24576
  47.7 5.0 all-to-all-start
  53.4 9.6 all-gather.12.cloned.1.call-done
  70.2 16.2 %all-to-all-done = bf16[3,256,768]{1,0,2:T(4,128)(2,1)S(1)} async-done(((bf16[3,256,768]{1,0,2:T(4,128)(2,1)}), bf16[3,256,768]{1,0,2:T(4,128)(2,1)S(1)}, u32[]{:S(2)}, u32[]{:S(2)}) %all-to-all-start) | async-done | bytes 1179680 | tf_op jit(solution)/shard_map/all_to_all | solution.py:170
  86.5 4.3 all-to-all-start.2
  98.7 28.6 %all-to-all-done.2 = bf16[3,256,768]{1,0,2:T(4,128)(2,1)} async-done(((bf16[3,256,768]{1,0,2:T(4,128)(2,1)}), bf16[3,256,768]{1,0,2:T(4,128)(2,1)}, u32[]{:S(2)}, u32[]{:S(2)}) %all-to-all-start.2) | async-done | bytes 1179680 | tf_op jit(solution)/shard_map/all_to_all | solution.py:184
  127.3 4.3 all-to-all-start.1
  132.3 41.2 %all_gather.56 = s32[3,1024]{1,0:T(4,128)S(1)} all-gather(s32[3,256]{1,0:T(4,128)S(1)} %copy-done.26), channel_id=1, replica_groups=mesh['dp'=8,'seq'=4] {'seq'}, dimensions={1}, use_global_device_ids=true | all-gather | bytes 15360 | tf_op jit(solution)/shard_map/all_gather | solution.py:156
  202.1 99.2 %while.26 = (s32[]{:T(128)}, bf16[9,1024,64]{1,2,0:T(8,128)(2,1)}, f32[9,1024]{1,0:T(8,128)}, s32[9,1024]{1,0:T(8,128)}, bf16[9,1024,64]{2,1,0:T(8,128)(2,1)S(1)...) while((s32[]{:T(128)}, bf16[9,1024,64]{1,2,0:T(8,128)(2,1)}, ...), condition=%wide.region_5.6_spmd, body=%wide.region_2.5_spmd.sunk | while | flops 284228608 | bytes 30349440 | solution.py:197
  208.9 4.2 fusion.156
  219.9 4.2 fusion.156
  231.0 4.2 fusion.156
  242.0 4.2 fusion.156
  253.0 4.2 fusion.156
  264.0 4.2 fusion.156
  275.0 4.2 fusion.156
  286.0 4.2 fusion.156
  297.1 4.2 fusion.156
  301.3 4.2 copy.112
  305.5 4.6 all-to-all-start.3
  311.4 10.1 all-gather
  322.1 33.6 %all-to-all-done.3 = bf16[3,1024,192]{2,0,1:T(4,128)(2,1)} async-done(((bf16[3,1024,192]{2,0,1:T(4,128)(2,1)}), bf16[3,1024,192]{2,0,1:T(4,128)(2,1)}, u32[]{:S(2)}, u32[]{:S(2)}) %all-to-all-start.3) | async-done | bytes 1179680 | tf_op jit(solution)/shard_map/all_to_all | solution.py:201
  364.3 27.2 %fusion.56 = (bf16[768,3072]{1,0:T(8,128)(2,1)}, f32[768,3072]{1,0:T(8,128)}) fusion(f32[3072]{0:T(1024)} %bitcast.275, bf16[768,3072]{1,0:T(8,128)(2,1)} %all-gather.16.cloned.1.call-done, f32[768,768]{1,0:T(8,128)S(1)} %get-tuple-element.265, f32[768]{0:T(1024)S(1)} %convert_element_type.227, f32[768]{0:T(1024)S(1)} %convert_element_type.226, ...), kind=kOutput, calls=%fused_computation.64 | convolution fusion | flops 3782541312 | bytes 21258240 | tf_op jit(solution)/shard_map/dot_general | solution.py:213
  391.5 11.6 %convert_reduce_fusion = (f32[3072]{0:T(1024)}, bf16[768,3072]{1,0:T(8,128)(2,1)S(1)}) fusion(f32[768,3072]{1,0:T(8,128)} %get-tuple-element.267, f32[3072]{0:T(1024)} %bitcast.276, bf16[768,768]{1,0:T(8,128)(2,1)} %bitcast.249, bf16[3072,768]{1,0:T(8,128)(2,1)} %all-gather.18.cloned.1.call-done), kind=kOutput, calls=%fused_computation.71 | convolution fusion | flops 3654546432 | bytes 20078592 | tf_op jit(solution)/shard_map/dot_general | solution.py:40
  403.2 4.8 multiply_reduce_fusion.1
  415.4 4.3 all-to-all-start.4
  419.8 4.5 fusion.90
  424.4 31.9 %all-to-all-done.4 = bf16[3,256,768]{1,0,2:T(4,128)(2,1)} async-done(((bf16[3,256,768]{1,0,2:T(4,128)(2,1)}), bf16[3,256,768]{1,0,2:T(4,128)(2,1)}, u32[]{:S(2)}, u32[]{:S(2)}) %all-to-all-start.4) | async-done | bytes 1179680 | tf_op jit(solution)/shard_map/all_to_all | solution.py:252
  467.1 124.2 %while.27 = (s32[]{:T(128)}, bf16[9,1024,64]{1,2,0:T(8,128)(2,1)}, bf16[9,1024,64]{1,2,0:T(8,128)(2,1)}, bf16[9,1024,64]{1,2,0:T(8,128)(2,1)}, s32[9,1024]{1,0:T...) while((s32[]{:T(128)}, bf16[9,1024,64]{1,2,0:T(8,128)(2,1)}, ...), condition=%wide.region_12.13_spmd, body=%wide.region_10.12_spmd.sunk | while | flops 681901056 | bytes 33465460 | solution.py:253
  595.3 4.4 all-to-all-start.5
  602.0 45.4 %all-to-all-done.5 = bf16[3,1024,192]{2,0,1:T(4,128)(2,1)} async-done(((bf16[3,1024,192]{2,0,1:T(4,128)(2,1)}), bf16[3,1024,192]{2,0,1:T(4,128)(2,1)}, u32[]{:S(2)}, u32[]{:S(2)}) %all-to-all-start.5) | async-done | bytes 1179680 | tf_op jit(solution)/shard_map/all_to_all | solution.py:265
  647.5 4.2 copy.124
  655.7 4.2 fusion.99
  660.0 4.1 copy.125
  664.0 51.4 %all_to_all.120 = bf16[3,1024,192]{2,0,1:T(4,128)(2,1)S(1)} all-to-all(bf16[3,1024,192]{2,0,1:T(4,128)(2,1)} %copy.125), channel_id=1, replica_groups=mesh['dp'=8,'seq'=4] {'seq'}, dimensions={1} | all-to-all | bytes 2359296 | tf_op jit(solution)/shard_map/all_to_all | solution.py:272
  722.1 4.2 fusion.100
  730.5 50.8 %all_to_all.121 = bf16[3,1024,192]{2,0,1:T(4,128)(2,1)S(1)} all-to-all(bf16[3,1024,192]{2,0,1:T(4,128)(2,1)} %copy.128), channel_id=1, replica_groups=mesh['dp'=8,'seq'=4] {'seq'}, dimensions={1} | all-to-all | bytes 2359296 | tf_op jit(solution)/shard_map/all_to_all | solution.py:279
  789.3 4.1 fusion.101
  793.5 9.0 fusion.93
  802.6 10.6 fusion.102
  817.2 8.6 add_convert_fusion
  825.8 4.4 copy.135
  839.9 4.1 fusion.97
  849.0 67.9 %reduce-scatter.15.cloned.1.call-done = f32[96,3072]{1,0:T(8,128)} async-done(((f32[768,3072]{1,0:T(8,128)}), f32[96,3072]{1,0:T(8,128)}) %reduce-scatter.15.cloned.1.call-update) | async-done | bytes 1179664 | tf_op jit(solution)/shard_map/reduce_scatter | solution.py:334
  919.0 77.7 %reduce-scatter.17.cloned.1.call-done = f32[384,768]{1,0:T(8,128)} async-done(((f32[3072,768]{1,0:T(8,128)}), f32[384,768]{1,0:T(8,128)}) %reduce-scatter.17.cloned.1.call-update) | async-done | bytes 1179664 | tf_op jit(solution)/shard_map/reduce_scatter | solution.py:336
  1005.2 26.3 %all-reduce.17 = (bf16[768]{0:T(1024)(128)(2,1)}, bf16[768]{0:T(1024)(128)(2,1)}, bf16[768]{0:T(1024)(128)(2,1)}, bf16[768]{0:T(1024)(128)(2,1)}, bf16[768]{0:T(...) all-reduce(f32[768]{0:T(1024)} %get-tuple-element.184, ...), channel_id=2, replica_groups=mesh['dp'=8,'seq'=4] {'dp'}, use_global_device_ids=true, to_apply=%region_16.17.clone | all-reduce | flops 9216 | bytes 55296
  1042.2 13.1 %all-reduce.19 = (bf16[96]{0:T(256)(128)(2,1)}, bf16[96]{0:T(256)(128)(2,1)}, bf16[96]{0:T(256)(128)(2,1)}, bf16[96]{0:T(256)(128)(2,1)}, bf16[96]{0:T(256)(128)...) all-reduce(bf16[96]{0:T(256)(128)(2,1)} %dynamic-slice.43, ...), channel_id=1, replica_groups=mesh['dp'=8,'seq'=4] {'seq'}, use_global_device_ids=true, to_apply=%region_17.18 | all-reduce | flops 1152 | bytes 4608 | tf_op jit(solution)/shard_map/psum | solution.py:356
  1070.8 8.2 all-reduce.23.cloned.1.call-done
  (382 shorter events, 362.9 us)
Async XLA Ops:
  7.2 4.9 copy-start.31
  7.2 34.9 %copy-start.1 = (bf16[3,256,768]{2,1,0:T(8,128)(2,1)S(1)}, bf16[3,256,768]{2,1,0:T(8,128)(2,1)}, u32[]{:S(2)}) copy-start(bf16[3,256,768]{2,1,0:T(8,128)(2,1)} %param.22) | copy-start | bytes 3538948
  7.2 6.1 copy-start.36
  7.2 6.4 copy-start.37
  7.2 6.6 copy-start.38
  7.2 6.8 copy-start.39
  7.3 7.0 copy-start.40
  7.3 7.3 copy-start.41
  7.3 7.5 copy-start.42
  7.3 7.7 copy-start.43
  7.3 35.4 %all-gather.8.cloned.1.call-start = ((), (), s32[]{:S(2)}) async-start(), calls=%async_computation.14 | async-start | bytes 1327104 | tf_op jit(solution)/shard_map/all_gather | solution.py:142
  8.0 54.9 %all-gather.12.cloned.1.call-start = ((), (), s32[]{:S(2)}) async-start(), calls=%async_computation.16 | async-start | bytes 1327104 | tf_op jit(solution)/shard_map/all_gather | solution.py:145
  10.3 31.3 %copy-start.18 = (f32[3,256]{1,0:T(4,128)}, f32[3,256]{1,0:T(4,128)S(1)}, u32[]{:S(2)}) copy-start(f32[3,256]{1,0:T(4,128)S(1)} %broadcast_multiply_fusion.5) | copy-start | bytes 9220
  12.1 30.6 %copy-start.19 = (f32[768]{0:T(1024)}, f32[768]{0:T(1024)S(1)}, u32[]{:S(2)}) copy-start(f32[768]{0:T(1024)S(1)} %div.35) | copy-start | bytes 9220
  47.7 38.8 %all-to-all-start = ((bf16[3,256,768]{1,0,2:T(4,128)(2,1)}), bf16[3,256,768]{1,0,2:T(4,128)(2,1)S(1)}, u32[]{:S(2)}, u32[]{:S(2)}) async-start(bf16[3,256,768]{1,0,2:T(4,128)(2,1)} %copy.100), calls=%async_computation | async-start | bytes 3145728 | tf_op jit(solution)/shard_map/all_to_all | solution.py:170
  52.6 38.8 %all-gather.10.cloned.1.call-start = ((), (), s32[]{:S(2)}) async-start(), calls=%async_computation.15 | async-start | bytes 1327104 | tf_op jit(solution)/shard_map/all_gather | solution.py:144
  86.5 40.9 %all-to-all-start.2 = ((bf16[3,256,768]{1,0,2:T(4,128)(2,1)}), bf16[3,256,768]{1,0,2:T(4,128)(2,1)}, u32[]{:S(2)}, u32[]{:S(2)}) async-start(bf16[3,256,768]{1,0,2:T(4,128)(2,1)} %copy.106), calls=%async_computation.2 | async-start | bytes 3145728 | tf_op jit(solution)/shard_map/all_to_all | solution.py:184
  90.8 270.2 %all-gather.14.cloned.1.call-start = ((), (), s32[]{:S(2)}) async-start(), calls=%async_computation.17 | async-start | bytes 1327104 | tf_op jit(solution)/shard_map/all_gather | solution.py:147
  98.7 33.6 %copy-start.26 = (s32[3,256]{1,0:T(4,128)S(1)}, s32[3,256]{1,0:T(4,128)}, u32[]{:S(2)}) copy-start(s32[3,256]{1,0:T(4,128)} %param.23) | copy-start | bytes 9220
  127.3 63.0 %all-to-all-start.1 = ((bf16[3,256,768]{1,0,2:T(4,128)(2,1)}), bf16[3,256,768]{1,0,2:T(4,128)(2,1)}, u32[]{:S(2)}, u32[]{:S(2)}) async-start(bf16[3,256,768]{1,0,2:T(4,128)(2,1)} %copy.103), calls=%async_computation.1 | async-start | bytes 3145728 | tf_op jit(solution)/shard_map/all_to_all | solution.py:177
  131.7 232.6 %all-gather.16.cloned.1.call-start = ((), (), s32[]{:S(2)}) async-start(), calls=%async_computation.18 | async-start | bytes 5308416 | tf_op jit(solution)/shard_map/all_gather | solution.py:151
  301.3 4.3 copy-start.4
  305.5 5.2 copy-start.30
  305.5 5.2 copy-start.29
  305.5 5.2 copy-start.28
  305.5 50.2 %all-to-all-start.3 = ((bf16[3,1024,192]{2,0,1:T(4,128)(2,1)}), bf16[3,1024,192]{2,0,1:T(4,128)(2,1)}, u32[]{:S(2)}, u32[]{:S(2)}) async-start(bf16[3,1024,192]{2,0,1:T(4,128)(2,1)} %copy.112), calls=%async_computation.3 | async-start | bytes 4194304 | tf_op jit(solution)/shard_map/all_to_all | solution.py:201
  310.1 81.4 %all-gather.18.cloned.1.call-start = ((), (), s32[]{:S(2)}) async-start(), calls=%async_computation.19 | async-start | bytes 5308416 | tf_op jit(solution)/shard_map/all_gather | solution.py:153
  391.5 11.6 %copy-start.32 = (bf16[768,3072]{1,0:T(8,128)(2,1)S(1)}, bf16[768,3072]{1,0:T(8,128)(2,1)}, u32[]{:S(2)}) copy-start(bf16[768,3072]{1,0:T(8,128)(2,1)} %all-gather.16.cloned.1.call-done) | copy-start | bytes 14155780
  403.2 4.8 copy-start.8
  403.2 4.8 copy-start.7
  415.4 40.9 %all-to-all-start.4 = ((bf16[3,256,768]{1,0,2:T(4,128)(2,1)}), bf16[3,256,768]{1,0,2:T(4,128)(2,1)}, u32[]{:S(2)}, u32[]{:S(2)}) async-start(bf16[3,256,768]{1,0,2:T(4,128)(2,1)} %copy.115), calls=%async_computation.4 | async-start | bytes 3145728 | tf_op jit(solution)/shard_map/all_to_all | solution.py:252
  419.8 418.5 %reduce-scatter.13.cloned.1.call-start = ((), (), s32[]{:S(2)}) async-start(), calls=%async_computation.23 | async-start | bytes 2654208 | tf_op jit(solution)/shard_map/reduce_scatter | solution.py:330
  595.3 52.1 %all-to-all-start.5 = ((bf16[3,1024,192]{2,0,1:T(4,128)(2,1)}), bf16[3,1024,192]{2,0,1:T(4,128)(2,1)}, u32[]{:S(2)}, u32[]{:S(2)}) async-start(bf16[3,1024,192]{2,0,1:T(4,128)(2,1)} %copy.122), calls=%async_computation.5 | async-start | bytes 4194304 | tf_op jit(solution)/shard_map/all_to_all | solution.py:265
  599.8 244.3 %reduce-scatter.7.cloned.1.call-start = ((), (), s32[]{:S(2)}) async-start(), calls=%async_computation.20 | async-start | bytes 2654208 | tf_op jit(solution)/shard_map/reduce_scatter | solution.py:325
  659.9 185.7 %reduce-scatter.9.cloned.1.call-start = ((), (), s32[]{:S(2)}) async-start(), calls=%async_computation.21 | async-start | bytes 2654208 | tf_op jit(solution)/shard_map/reduce_scatter | solution.py:327
  726.4 120.9 %reduce-scatter.11.cloned.1.call-start = ((), (), s32[]{:S(2)}) async-start(), calls=%async_computation.22 | async-start | bytes 2654208 | tf_op jit(solution)/shard_map/reduce_scatter | solution.py:328
  793.5 123.4 %reduce-scatter.15.cloned.1.call-start = ((), (), s32[]{:S(2)}) async-start(), calls=%async_computation.24 | async-start | bytes 10616832 | tf_op jit(solution)/shard_map/reduce_scatter | solution.py:334
  802.5 194.2 %reduce-scatter.17.cloned.1.call-start = ((), (), s32[]{:S(2)}) async-start(), calls=%async_computation.25 | async-start | bytes 10616832 | tf_op jit(solution)/shard_map/reduce_scatter | solution.py:336
  813.2 265.8 %all-reduce.23.cloned.1.call-start = ((), (), s32[]{:S(2)}) async-start(), calls=%async_computation.26 | async-start | bytes 3538944 | tf_op jit(solution)/shard_map/psum | solution.py:358
  825.8 7.0 copy-start.3
  849.0 149.9 %copy-start.10 = (bf16[768,768]{1,0:T(8,128)(2,1)S(1)}, bf16[768,768]{1,0:T(8,128)(2,1)}, u32[]{:S(2)}) copy-start(bf16[768,768]{1,0:T(8,128)(2,1)} %reshape.310) | copy-start | bytes 3538948
  849.0 149.9 %copy-start.34 = (bf16[768,768]{1,0:T(8,128)(2,1)S(1)}, bf16[768,768]{1,0:T(8,128)(2,1)}, u32[]{:S(2)}) copy-start(bf16[768,768]{1,0:T(8,128)(2,1)} %all-gather.10.cloned.1.call-done) | copy-start | bytes 3538948
  1001.3 3.8 copy-start.25
  1001.3 65.9 %copy-start.6 = (f32[768,768]{1,0:T(8,128)S(1)}, f32[768,768]{1,0:T(8,128)}, u32[]{:S(2)}) copy-start(f32[768,768]{1,0:T(8,128)} %copy-done.5) | copy-start | bytes 7077892
  1079.0 4.4 copy-start.15
  1079.0 5.1 copy-start.14
  1079.0 5.9 copy-start.13
  1079.0 6.6 copy-start.12
  (24 other events, 40.0 us)
Sparse Core Ops, SparseCore 0:
  10.0 26.8 all-gather.7
  38.8 24.0 all-gather.11
  64.8 24.0 all-gather.9
  93.2 26.1 all-gather.13
  134.1 41.8 all-gather.15
  312.5 41.8 all-gather.17
  424.5 45.4 reduce-scatter.12
  660.0 43.1 reduce-scatter.6
  726.5 43.1 reduce-scatter.8
  793.6 43.2 reduce-scatter.10
  840.4 76.4 reduce-scatter.14
  920.2 76.4 reduce-scatter.16
  1000.7 78.2 all-reduce.22
where the time goes:
time: 1110 us; the launch traced here: 1090 us
  waiting for transfers between devices  323 us (29%)
  matrix products  266 us (24%)
  blocking collectives  219 us (20%)
  local copies, waits for them, and re-layouts  172 us (15%)
  other arithmetic  68 us (6%)
  starting transfers between devices  27.7 us (2%)
  between operations  16.7 us (2%)
    reduce_scatter x1, waiting for transfers between devices, per_device(): lax.psum_scatter(d_w_down, 'dp', scatter_dimension=0, tiled=True)  77.7 us
    reduce_scatter x1, waiting for transfers between devices, per_device(): lax.psum_scatter(d_w_up, 'dp', scatter_dimension=0, tiled=True)  67.9 us
    unnamed x2, blocking collectives  52.5 us
    all_to_all x1, blocking collectives, per_device(): lax.all_to_all(from_pairs(grad_key_pairs, seqs_here, heads_here), 'seq',...  51.4 us
    all_to_all x1, blocking collectives, per_device(): lax.all_to_all(from_pairs(grad_value_pairs, seqs_here, heads_here), 'seq'...  50.8 us
    all_to_all x1, waiting for transfers between devices, per_device(): lax.all_to_all(from_pairs(grad_query_pairs, seqs_here, heads_here), 'seq'...  45.4 us
    all_gather x1, blocking collectives, per_device(): full_segments = lax.all_gather(segment_ids, 'seq', axis=1, tiled=True)  41.2 us
    dot_general x18, matrix products, masked_scores(): jnp.einsum('qd,kd->qk', query_pair, key_pair, preferred_element_type=jnp....  38.3 us
  transfers between devices with their start and end apart: 19, of which 9 were waited for; matrix products, arithmetic and copies ran while one was open for 41% of the time, Pallas kernels for 0%

commit v1 on v0

--- a/solution.py
+++ b/solution.py
@@ -198,9 +198,16 @@
         attend_forward, (query_pairs, key_pairs, value_pairs, segment_pairs)
     )
     attn_heads = from_pairs(attn_pairs, seqs_here, heads_here)
-    attn_tok = lax.all_to_all(attn_heads, "seq", split_axis=1, concat_axis=2, tiled=True).reshape(
-        token_rows, model_width
-    )
+    switch_the_outputs = lambda payload: jnp.concatenate(
+        lax.all_to_all(
+            jnp.stack(jnp.split(payload, lax.axis_size("seq"), axis=1)),
+            axis_name="seq",
+            split_axis=0,
+            concat_axis=0,
+        ),
+        axis=2,
+    )
+    attn_tok = switch_the_outputs(attn_heads).reshape(token_rows, model_width)
     middle = (
         flat_in
         + jnp.dot(attn_tok, w_out, preferred_element_type=jnp.float32)

time: 1110 us -> 1090 us (0.982)
  waiting for transfers between devices: 323 us -> 304 us
    all_to_all x1, waiting for transfers between devices: 33.6 us -> 14.2 us  [per_device(): lax.all_to_all(jnp.stack(jnp.split(payload, lax.axis_size('seq'), axis=1)...]
  transfers between devices with their start and end apart: 19 -> 19, of which waited for: 9 -> 9; matrix products, arithmetic and copies ran while one was open for 41% -> 42% of each run, Pallas kernels for 0% -> 0%
where the time goes in v1:
time: 1090 us; the launch traced here: 1070 us
  waiting for transfers between devices  304 us (28%)
  matrix products  266 us (24%)
  blocking collectives  219 us (20%)
  local copies, waits for them, and re-layouts  171 us (16%)
  other arithmetic  69.1 us (6%)
  starting transfers between devices  26.8 us (2%)
  between operations  16.9 us (2%)
    reduce_scatter x1, waiting for transfers between devices, per_device(): lax.psum_scatter(d_w_down, 'dp', scatter_dimension=0, tiled=True)  77.7 us
    reduce_scatter x1, waiting for transfers between devices, per_device(): lax.psum_scatter(d_w_up, 'dp', scatter_dimension=0, tiled=True)  67.7 us
    unnamed x2, blocking collectives  52.5 us
    all_to_all x1, blocking collectives, per_device(): lax.all_to_all(from_pairs(grad_key_pairs, seqs_here, heads_here), 'seq',...  51.5 us
    all_to_all x1, blocking collectives, per_device(): lax.all_to_all(from_pairs(grad_value_pairs, seqs_here, heads_here), 'seq'...  50.8 us
    all_to_all x1, waiting for transfers between devices, per_device(): lax.all_to_all(from_pairs(grad_query_pairs, seqs_here, heads_here), 'seq'...  45.5 us
    all_gather x1, blocking collectives, per_device(): full_segments = lax.all_gather(segment_ids, 'seq', axis=1, tiled=True)  41.2 us
    dot_general x18, matrix products, masked_scores(): jnp.einsum('qd,kd->qk', query_pair, key_pair, preferred_element_type=jnp....  38.3 us
  transfers between devices with their start and end apart: 19, of which 9 were waited for; matrix products, arithmetic and copies ran while one was open for 42% of the time, Pallas kernels for 0%

profile of v1, /device:TPU:0, one launch (start us, length us, event | category | flops | bytes accessed | tf_op | source)
XLA Modules:
  0.0 1073.0 jit_solution(4321748159664221893)
XLA Ops:
  15.2 26.3 %all-reduce.18 = (bf16[768]{0:T(1024)(128)(2,1)S(1)}, bf16[768]{0:T(1024)(128)(2,1)S(1)}, bf16[768]{0:T(1024)(128)(2,1)S(1)}, bf16[768]{0:T(1024)(128)(2,1)S(1)}...) all-reduce(bf16[768]{0:T(1024)(128)(2,1)S(1)} %dynamic-update-slice, ...), channel_id=1, replica_groups=mesh['dp'=8,'seq'=4] {'dp'}, use_global_device_ids=true, to_apply=%add.1 | all-reduce | flops 6144 | bytes 24576
  47.7 5.0 all-to-all-start
  53.4 9.6 all-gather.12.cloned.1.call-done
  70.2 16.2 %all-to-all-done = bf16[3,256,768]{1,0,2:T(4,128)(2,1)S(1)} async-done(((bf16[3,256,768]{1,0,2:T(4,128)(2,1)}), bf16[3,256,768]{1,0,2:T(4,128)(2,1)S(1)}, u32[]{:S(2)}, u32[]{:S(2)}) %all-to-all-start) | async-done | bytes 1179680 | tf_op jit(solution)/shard_map/all_to_all | solution.py:170
  86.5 4.3 all-to-all-start.2
  98.7 28.6 %all-to-all-done.2 = bf16[3,256,768]{1,0,2:T(4,128)(2,1)} async-done(((bf16[3,256,768]{1,0,2:T(4,128)(2,1)}), bf16[3,256,768]{1,0,2:T(4,128)(2,1)}, u32[]{:S(2)}, u32[]{:S(2)}) %all-to-all-start.2) | async-done | bytes 1179680 | tf_op jit(solution)/shard_map/all_to_all | solution.py:184
  127.3 4.3 all-to-all-start.1
  132.3 41.2 %all_gather.56 = s32[3,1024]{1,0:T(4,128)S(1)} all-gather(s32[3,256]{1,0:T(4,128)S(1)} %copy-done.27), channel_id=1, replica_groups=mesh['dp'=8,'seq'=4] {'seq'}, dimensions={1}, use_global_device_ids=true | all-gather | bytes 15360 | tf_op jit(solution)/shard_map/all_gather | solution.py:156
  202.1 99.2 %while.26 = (s32[]{:T(128)}, bf16[9,1024,64]{1,2,0:T(8,128)(2,1)}, f32[9,1024]{1,0:T(8,128)}, s32[9,1024]{1,0:T(8,128)}, bf16[9,1024,64]{2,1,0:T(8,128)(2,1)S(1)...) while((s32[]{:T(128)}, bf16[9,1024,64]{1,2,0:T(8,128)(2,1)}, ...), condition=%wide.region_5.6_spmd, body=%wide.region_2.5_spmd.sunk | while | flops 284228608 | bytes 30349440 | solution.py:197
  208.9 4.2 fusion.156
  219.9 4.2 fusion.156
  231.0 4.2 fusion.156
  242.0 4.2 fusion.156
  253.0 4.2 fusion.156
  264.0 4.2 fusion.156
  275.1 4.2 fusion.156
  286.1 4.2 fusion.156
  297.1 4.2 fusion.156
  309.7 10.1 all-gather
  320.4 14.2 %all-to-all-done.3 = bf16[4,3,256,192]{2,3,1,0:T(8,128)(2,1)S(1)} async-done(((bf16[4,3,256,192]{2,3,1,0:T(8,128)(2,1)}), bf16[4,3,256,192]{2,3,1,0:T(8,128)(2,1)S(1)}, u32[]{:S(2)}, u32[]{:S(2)}) %all-to-all-start.3) | async-done | bytes 1179680 | tf_op jit(solution)/shard_map/all_to_all | solution.py:202
  343.9 27.3 %fusion.56 = (bf16[768,3072]{1,0:T(8,128)(2,1)}, f32[768,3072]{1,0:T(8,128)}) fusion(f32[3072]{0:T(1024)} %bitcast.281, bf16[768,3072]{1,0:T(8,128)(2,1)} %all-gather.16.cloned.1.call-done, f32[768,768]{1,0:T(8,128)S(1)} %get-tuple-element.269, f32[768]{0:T(1024)S(1)} %convert_element_type.227, f32[768]{0:T(1024)S(1)} %convert_element_type.226, ...), kind=kOutput, calls=%fused_computation.64 | convolution fusion | flops 3782541312 | bytes 21258240 | tf_op jit(solution)/shard_map/dot_general | solution.py:220
  371.2 11.9 %convert_reduce_fusion = (f32[3072]{0:T(1024)}, bf16[768,3072]{1,0:T(8,128)(2,1)S(1)}) fusion(f32[768,3072]{1,0:T(8,128)} %get-tuple-element.271, f32[3072]{0:T(1024)} %bitcast.282, bf16[768,768]{1,0:T(8,128)(2,1)} %bitcast.254, bf16[3072,768]{1,0:T(8,128)(2,1)} %all-gather.18.cloned.1.call-done), kind=kOutput, calls=%fused_computation.71 | convolution fusion | flops 3654546432 | bytes 20078592 | tf_op jit(solution)/shard_map/dot_general | solution.py:40
  383.1 4.8 multiply_reduce_fusion.1
  395.3 4.4 all-to-all-start.4
  399.8 4.5 fusion.90
  404.3 31.9 %all-to-all-done.4 = bf16[3,256,768]{1,0,2:T(4,128)(2,1)} async-done(((bf16[3,256,768]{1,0,2:T(4,128)(2,1)}), bf16[3,256,768]{1,0,2:T(4,128)(2,1)}, u32[]{:S(2)}, u32[]{:S(2)}) %all-to-all-start.4) | async-done | bytes 1179680 | tf_op jit(solution)/shard_map/all_to_all | solution.py:259
  446.8 124.2 %while.27 = (s32[]{:T(128)}, bf16[9,1024,64]{1,2,0:T(8,128)(2,1)}, bf16[9,1024,64]{1,2,0:T(8,128)(2,1)}, bf16[9,1024,64]{1,2,0:T(8,128)(2,1)}, s32[9,1024]{1,0:T...) while((s32[]{:T(128)}, bf16[9,1024,64]{1,2,0:T(8,128)(2,1)}, ...), condition=%wide.region_12.13_spmd, body=%wide.region_10.12_spmd.sunk | while | flops 681901056 | bytes 33465460 | solution.py:260
  571.0 4.1 copy.122
  575.1 4.4 all-to-all-start.5
  581.8 45.5 %all-to-all-done.5 = bf16[3,1024,192]{2,0,1:T(4,128)(2,1)} async-done(((bf16[3,1024,192]{2,0,1:T(4,128)(2,1)}), bf16[3,1024,192]{2,0,1:T(4,128)(2,1)}, u32[]{:S(2)}, u32[]{:S(2)}) %all-to-all-start.5) | async-done | bytes 1179680 | tf_op jit(solution)/shard_map/all_to_all | solution.py:272
  627.2 4.2 copy.124
  635.5 4.2 fusion.99
  639.7 4.1 copy.125
  643.8 51.5 %all_to_all.110 = bf16[3,1024,192]{2,0,1:T(4,128)(2,1)S(1)} all-to-all(bf16[3,1024,192]{2,0,1:T(4,128)(2,1)} %copy.125), channel_id=1, replica_groups=mesh['dp'=8,'seq'=4] {'seq'}, dimensions={1} | all-to-all | bytes 2359296 | tf_op jit(solution)/shard_map/all_to_all | solution.py:279
  702.0 4.2 fusion.100
  706.2 4.0 copy.128
  710.3 50.8 %all_to_all.111 = bf16[3,1024,192]{2,0,1:T(4,128)(2,1)S(1)} all-to-all(bf16[3,1024,192]{2,0,1:T(4,128)(2,1)} %copy.128), channel_id=1, replica_groups=mesh['dp'=8,'seq'=4] {'seq'}, dimensions={1} | all-to-all | bytes 2359296 | tf_op jit(solution)/shard_map/all_to_all | solution.py:286
  769.1 4.1 fusion.101
  773.4 9.0 fusion.93
  782.4 10.6 fusion.102
  797.0 8.6 add_convert_fusion
  805.6 4.4 copy.133
  819.7 4.1 fusion.97
  828.8 67.7 %reduce-scatter.15.cloned.1.call-done = f32[96,3072]{1,0:T(8,128)} async-done(((f32[768,3072]{1,0:T(8,128)}), f32[96,3072]{1,0:T(8,128)}) %reduce-scatter.15.cloned.1.call-update) | async-done | bytes 1179664 | tf_op jit(solution)/shard_map/reduce_scatter | solution.py:341
  898.7 77.7 %reduce-scatter.17.cloned.1.call-done = f32[384,768]{1,0:T(8,128)} async-done(((f32[3072,768]{1,0:T(8,128)}), f32[384,768]{1,0:T(8,128)}) %reduce-scatter.17.cloned.1.call-update) | async-done | bytes 1179664 | tf_op jit(solution)/shard_map/reduce_scatter | solution.py:343
  984.9 26.2 %all-reduce.17 = (bf16[768]{0:T(1024)(128)(2,1)}, bf16[768]{0:T(1024)(128)(2,1)}, bf16[768]{0:T(1024)(128)(2,1)}, bf16[768]{0:T(1024)(128)(2,1)}, bf16[768]{0:T(...) all-reduce(f32[768]{0:T(1024)} %get-tuple-element.184, ...), channel_id=2, replica_groups=mesh['dp'=8,'seq'=4] {'dp'}, use_global_device_ids=true, to_apply=%region_16.17.clone | all-reduce | flops 9216 | bytes 55296
  1021.8 13.1 %all-reduce.19 = (bf16[96]{0:T(256)(128)(2,1)}, bf16[96]{0:T(256)(128)(2,1)}, bf16[96]{0:T(256)(128)(2,1)}, bf16[96]{0:T(256)(128)(2,1)}, bf16[96]{0:T(256)(128)...) all-reduce(bf16[96]{0:T(256)(128)(2,1)} %dynamic-slice.43, ...), channel_id=1, replica_groups=mesh['dp'=8,'seq'=4] {'seq'}, use_global_device_ids=true, to_apply=%region_17.18 | all-reduce | flops 1152 | bytes 4608 | tf_op jit(solution)/shard_map/psum | solution.py:363
  1050.3 8.3 all-reduce.23.cloned.1.call-done
  (385 shorter events, 362.2 us)
Async XLA Ops:
  7.2 4.9 copy-start.32
  7.2 34.9 %copy-start.1 = (bf16[3,256,768]{2,1,0:T(8,128)(2,1)S(1)}, bf16[3,256,768]{2,1,0:T(8,128)(2,1)}, u32[]{:S(2)}) copy-start(bf16[3,256,768]{2,1,0:T(8,128)(2,1)} %param.22) | copy-start | bytes 3538948
  7.2 6.1 copy-start.37
  7.2 6.4 copy-start.38
  7.2 6.6 copy-start.39
  7.2 6.8 copy-start.40
  7.3 7.0 copy-start.41
  7.3 7.3 copy-start.42
  7.3 7.5 copy-start.43
  7.3 7.7 copy-start.44
  7.3 35.4 %all-gather.8.cloned.1.call-start = ((), (), s32[]{:S(2)}) async-start(), calls=%async_computation.14 | async-start | bytes 1327104 | tf_op jit(solution)/shard_map/all_gather | solution.py:142
  8.0 54.9 %all-gather.12.cloned.1.call-start = ((), (), s32[]{:S(2)}) async-start(), calls=%async_computation.16 | async-start | bytes 1327104 | tf_op jit(solution)/shard_map/all_gather | solution.py:145
  10.3 31.3 %copy-start.19 = (f32[3,256]{1,0:T(4,128)}, f32[3,256]{1,0:T(4,128)S(1)}, u32[]{:S(2)}) copy-start(f32[3,256]{1,0:T(4,128)S(1)} %broadcast_multiply_fusion.5) | copy-start | bytes 9220
  12.1 30.6 %copy-start.20 = (f32[768]{0:T(1024)}, f32[768]{0:T(1024)S(1)}, u32[]{:S(2)}) copy-start(f32[768]{0:T(1024)S(1)} %div.35) | copy-start | bytes 9220
  47.7 38.8 %all-to-all-start = ((bf16[3,256,768]{1,0,2:T(4,128)(2,1)}), bf16[3,256,768]{1,0,2:T(4,128)(2,1)S(1)}, u32[]{:S(2)}, u32[]{:S(2)}) async-start(bf16[3,256,768]{1,0,2:T(4,128)(2,1)} %copy.102), calls=%async_computation | async-start | bytes 3145728 | tf_op jit(solution)/shard_map/all_to_all | solution.py:170
  52.6 38.8 %all-gather.10.cloned.1.call-start = ((), (), s32[]{:S(2)}) async-start(), calls=%async_computation.15 | async-start | bytes 1327104 | tf_op jit(solution)/shard_map/all_gather | solution.py:144
  86.5 40.9 %all-to-all-start.2 = ((bf16[3,256,768]{1,0,2:T(4,128)(2,1)}), bf16[3,256,768]{1,0,2:T(4,128)(2,1)}, u32[]{:S(2)}, u32[]{:S(2)}) async-start(bf16[3,256,768]{1,0,2:T(4,128)(2,1)} %copy.108), calls=%async_computation.2 | async-start | bytes 3145728 | tf_op jit(solution)/shard_map/all_to_all | solution.py:184
  90.8 249.9 %all-gather.14.cloned.1.call-start = ((), (), s32[]{:S(2)}) async-start(), calls=%async_computation.17 | async-start | bytes 1327104 | tf_op jit(solution)/shard_map/all_gather | solution.py:147
  98.7 33.6 %copy-start.27 = (s32[3,256]{1,0:T(4,128)S(1)}, s32[3,256]{1,0:T(4,128)}, u32[]{:S(2)}) copy-start(s32[3,256]{1,0:T(4,128)} %param.23) | copy-start | bytes 9220
  127.3 63.0 %all-to-all-start.1 = ((bf16[3,256,768]{1,0,2:T(4,128)(2,1)}), bf16[3,256,768]{1,0,2:T(4,128)(2,1)}, u32[]{:S(2)}, u32[]{:S(2)}) async-start(bf16[3,256,768]{1,0,2:T(4,128)(2,1)} %copy.105), calls=%async_computation.1 | async-start | bytes 3145728 | tf_op jit(solution)/shard_map/all_to_all | solution.py:177
  131.7 212.3 %all-gather.16.cloned.1.call-start = ((), (), s32[]{:S(2)}) async-start(), calls=%async_computation.18 | async-start | bytes 5308416 | tf_op jit(solution)/shard_map/all_gather | solution.py:151
  301.3 3.4 copy-start.4
  303.5 5.4 copy-start.31
  303.5 5.4 copy-start.30
  303.5 5.4 copy-start.29
  304.7 30.0 %all-to-all-start.3 = ((bf16[4,3,256,192]{2,3,1,0:T(8,128)(2,1)}), bf16[4,3,256,192]{2,3,1,0:T(8,128)(2,1)S(1)}, u32[]{:S(2)}, u32[]{:S(2)}) async-start(bf16[4,3,256,192]{2,3,1,0:T(8,128)(2,1)} %pad_maximum_fusion), calls=%async_computation.3 | async-start | bytes 2359296 | tf_op jit(solution)/shard_map/all_to_all | solution.py:202
  308.4 62.9 %all-gather.18.cloned.1.call-start = ((), (), s32[]{:S(2)}) async-start(), calls=%async_computation.19 | async-start | bytes 5308416 | tf_op jit(solution)/shard_map/all_gather | solution.py:153
  371.2 11.9 %copy-start.33 = (bf16[768,3072]{1,0:T(8,128)(2,1)S(1)}, bf16[768,3072]{1,0:T(8,128)(2,1)}, u32[]{:S(2)}) copy-start(bf16[768,3072]{1,0:T(8,128)(2,1)} %all-gather.16.cloned.1.call-done) | copy-start | bytes 14155780
  383.1 4.8 copy-start.9
  383.1 4.8 copy-start.7
  395.3 40.9 %all-to-all-start.4 = ((bf16[3,256,768]{1,0,2:T(4,128)(2,1)}), bf16[3,256,768]{1,0,2:T(4,128)(2,1)}, u32[]{:S(2)}, u32[]{:S(2)}) async-start(bf16[3,256,768]{1,0,2:T(4,128)(2,1)} %copy.115), calls=%async_computation.4 | async-start | bytes 3145728 | tf_op jit(solution)/shard_map/all_to_all | solution.py:259
  399.7 418.4 %reduce-scatter.13.cloned.1.call-start = ((), (), s32[]{:S(2)}) async-start(), calls=%async_computation.23 | async-start | bytes 2654208 | tf_op jit(solution)/shard_map/reduce_scatter | solution.py:337
  575.1 52.2 %all-to-all-start.5 = ((bf16[3,1024,192]{2,0,1:T(4,128)(2,1)}), bf16[3,1024,192]{2,0,1:T(4,128)(2,1)}, u32[]{:S(2)}, u32[]{:S(2)}) async-start(bf16[3,1024,192]{2,0,1:T(4,128)(2,1)} %copy.122), calls=%async_computation.5 | async-start | bytes 4194304 | tf_op jit(solution)/shard_map/all_to_all | solution.py:272
  579.5 244.3 %reduce-scatter.7.cloned.1.call-start = ((), (), s32[]{:S(2)}) async-start(), calls=%async_computation.20 | async-start | bytes 2654208 | tf_op jit(solution)/shard_map/reduce_scatter | solution.py:332
  639.7 185.8 %reduce-scatter.9.cloned.1.call-start = ((), (), s32[]{:S(2)}) async-start(), calls=%async_computation.21 | async-start | bytes 2654208 | tf_op jit(solution)/shard_map/reduce_scatter | solution.py:334
  706.2 120.9 %reduce-scatter.11.cloned.1.call-start = ((), (), s32[]{:S(2)}) async-start(), calls=%async_computation.22 | async-start | bytes 2654208 | tf_op jit(solution)/shard_map/reduce_scatter | solution.py:335
  773.3 123.3 %reduce-scatter.15.cloned.1.call-start = ((), (), s32[]{:S(2)}) async-start(), calls=%async_computation.24 | async-start | bytes 10616832 | tf_op jit(solution)/shard_map/reduce_scatter | solution.py:341
  782.4 194.0 %reduce-scatter.17.cloned.1.call-start = ((), (), s32[]{:S(2)}) async-start(), calls=%async_computation.25 | async-start | bytes 10616832 | tf_op jit(solution)/shard_map/reduce_scatter | solution.py:343
  793.0 265.7 %all-reduce.23.cloned.1.call-start = ((), (), s32[]{:S(2)}) async-start(), calls=%async_computation.26 | async-start | bytes 3538944 | tf_op jit(solution)/shard_map/psum | solution.py:365
  805.6 7.0 copy-start.3
  828.8 149.8 %copy-start.11 = (bf16[768,768]{1,0:T(8,128)(2,1)S(1)}, bf16[768,768]{1,0:T(8,128)(2,1)}, u32[]{:S(2)}) copy-start(bf16[768,768]{1,0:T(8,128)(2,1)} %reshape.309) | copy-start | bytes 3538948
  828.8 149.8 %copy-start.35 = (bf16[768,768]{1,0:T(8,128)(2,1)S(1)}, bf16[768,768]{1,0:T(8,128)(2,1)}, u32[]{:S(2)}) copy-start(bf16[768,768]{1,0:T(8,128)(2,1)} %all-gather.10.cloned.1.call-done) | copy-start | bytes 3538948
  981.0 3.8 copy-start.26
  981.0 65.8 %copy-start.6 = (f32[768,768]{1,0:T(8,128)S(1)}, f32[768,768]{1,0:T(8,128)}, u32[]{:S(2)}) copy-start(f32[768,768]{1,0:T(8,128)} %copy-done.5) | copy-start | bytes 7077892
  1058.7 4.4 copy-start.16
  1058.7 5.1 copy-start.15
  1058.7 5.9 copy-start.14
  1058.7 6.6 copy-start.13
  (25 other events, 41.1 us)
Sparse Core Ops, SparseCore 0:
  10.0 26.8 all-gather.7
  38.8 24.0 all-gather.11
  64.8 24.0 all-gather.9
  93.2 26.1 all-gather.13
  134.1 41.7 all-gather.15
  310.8 41.9 all-gather.17
  404.5 45.2 reduce-scatter.12
  639.8 43.0 reduce-scatter.6
  706.3 43.0 reduce-scatter.8
  773.4 43.0 reduce-scatter.10
  820.0 76.4 reduce-scatter.14
  899.9 76.4 reduce-scatter.16
  980.4 78.1 all-reduce.22
